TPU v7x, 32 devices: a whole 2x2x4 slice. The times are simulated.
32 devices in a mesh: row: 8 (over z, y), col: 4 (over x, core).
Axes of the slice: x: 2, y: 2, z: 4, core: 2. Of those that a mesh axis runs over, the one named last changes fastest.
Arguments:
- entries: int32 [32, 16, 128, 128], P('row', 'col'), may hold values from -2 to 2
- tile_cols: int32 [32, 16], P('row', 'col'), may hold values from 0 to 31
- block_now: int32 [32, 16384], P(None, ('col', 'row')), may hold values from 0 to 65520
- block_prev: int32 [32, 16384], P(None, ('col', 'row')), may hold values from 0 to 65520
- block_prev2: int32 [32, 16384], P(None, ('col', 'row')), may hold values from 0 to 65520
- gram_prev: int32 [32, 32], replicated, may hold values from 0 to 65520
- square_prev: int32 [32, 32], replicated, may hold values from 0 to 65520
- inverse_prev: int32 [32, 32], replicated, may hold values from 0 to 65520
- inverse_prev2: int32 [32, 32], replicated, may hold values from 0 to 65520
Outputs:
- next_block: float32 [32, 16384], P(None, ('col', 'row'))
- later_block: float32 [32, 16384], P(None, ('col', 'row'))
Inputs may be any that keep to these rules, and one draw needn't show every extreme that they name: `tile_cols`: stored tiles that name the same tile column in one tile row add. `block_prev`: residues. `block_prev2`: residues. `gram_prev`: residues. `square_prev`: residues. `inverse_prev`: residues. `inverse_prev2`: residues.
All inputs are finite; a program needn't handle non-finite values.
Results may differ from a plain program's by a relative error of at most 0.0003.
Values sent between devices are 32-bit elements; how exact they have to be, the bound alone decides.
A program may use at most 64 MiB of HBM per device.

v0:
```python
import functools

import jax
import jax.numpy as jnp
from jax import lax
from jax.experimental import pallas as pl
from jax.experimental.pallas import tpu as pltpu
from jax.sharding import PartitionSpec as P

modulus = 65521.0
reciprocal = 1.0 / 65521.0
MESH = pl.DeviceIdType.MESH
GATHER, PARTIAL, SCATTER, GRAM, SQUARE_ROW, SQUARE_COL = range(6)


def near(values):
    return values - jnp.floor(values * reciprocal + 0.5) * modulus


def whole(values):
    signed = near(values)
    return jnp.where(signed < 0.0, signed + modulus, signed)


def split(values):
    top = jnp.floor(values * (1.0 / 256.0) + 0.5)
    return top, values - top * 256.0


def digits(values):
    top, low = split(values)
    return jnp.concatenate([top, low], axis=0).astype(jnp.bfloat16)


def fold_two(top, low):
    return near(near(top) * 256.0 + low)


def fold_three(upper, middle, lower):
    return near(near(upper) * 15.0 + near(middle) * 256.0 + near(lower))


def mulmod(left, right):
    top, low = split(right)
    return near(near(left * top) * 256.0 + left * low)


def dot(left, right):
    return jnp.dot(left, right, preferred_element_type=jnp.float32)


def dot_t(left, right):
    return lax.dot_general(
        left, right, (((1,), (1,)), ((), ())), preferred_element_type=jnp.float32
    )


def product_parts(left, right):
    order = left.shape[0]
    left_digits = digits(left)
    right_top, right_low = split(right)
    with_top = dot(left_digits, right_top.astype(jnp.bfloat16))
    with_low = dot(left_digits, right_low.astype(jnp.bfloat16))
    return with_top[:order], with_top[order:] + with_low[:order], with_low[order:]


def small_product(left, right):
    return fold_three(*product_parts(left, right))


def gram_tiles(tiles):
    order = tiles[0].shape[0]
    total = None
    for tile in tiles:
        both = digits(tile)
        term = dot_t(both, both)
        total = term if total is None else total + term
    return fold_three(
        total[:order, :order],
        total[:order, order:] + total[order:, :order],
        total[order:, order:],
    )


def power_inverse(number):
    result = None
    square = number
    for position in range(16):
        if 65519 >> position & 1:
            result = square if result is None else mulmod(result, square)
        if position < 15:
            square = mulmod(square, square)
    return result


def identity_of(order):
    rows = lax.broadcasted_iota(jnp.int32, (order, order), 0)
    lanes = lax.broadcasted_iota(jnp.int32, (order, order), 1)
    return jnp.where(rows == lanes, 1.0, 0.0).astype(jnp.float32)


def inverse_of(matrix):
    order = matrix.shape[0]
    work = jnp.concatenate([matrix, identity_of(order)], axis=1)
    rows = lax.broadcasted_iota(jnp.int32, (order, 1), 0)
    for column in range(order):
        entry = work[:, column : column + 1]
        usable = (entry != 0.0) & (rows >= column)
        first = jnp.min(jnp.where(usable, rows, order), axis=0, keepdims=True)
        chosen = rows == jnp.where(first == order, column, first)
        pivot_row = jnp.sum(jnp.where(chosen, work, 0.0), axis=0, keepdims=True)
        pivot = jnp.sum(jnp.where(chosen, entry, 0.0), axis=0, keepdims=True)
        swapped = jnp.where(chosen, work[column : column + 1, :], work)
        factor = jnp.where(chosen, entry[column : column + 1, :], entry)
        pivot_row = jnp.where(pivot == 0.0, 0.0, pivot_row)
        pivot = jnp.where(pivot == 0.0, 1.0, pivot)
        pivot_top, pivot_low = split(pivot)
        factor_top, factor_low = split(factor)
        upper = near(pivot_top * swapped - factor_top * pivot_row)
        reduced = near(upper * 256.0 + (pivot_low * swapped - factor_low * pivot_row))
        work = jnp.where(rows == column, pivot_row, reduced)
    left = work[:, :order]
    diagonal = jnp.sum(left * identity_of(order), axis=1, keepdims=True)
    return mulmod(work[:, order:], power_inverse(diagonal))


def pack(values):
    rows = values.shape[0] // 4
    return jnp.concatenate([values[g * rows : (g + 1) * rows] for g in range(4)], axis=1)


def unpack(values):
    width = values.shape[1] // 4
    return jnp.concatenate([values[:, g * width : (g + 1) * width] for g in range(4)], axis=0)


def flipped(place, mask, count):
    assert count & (count - 1) == 0
    bit = 1
    moved = place
    while bit < count:
        if mask & bit:
            moved = moved + bit - 2 * bit * lax.rem(place // bit, 2)
        bit *= 2
    return moved


def kernel(
    n_row, n_col, cols_ref,
    entries_ref, now_ref, prev_ref, prev2_ref,
    gram_ref, square_ref, inverse_ref, inverse2_ref, next_ref, later_ref,
    tile16, full_a, full_b, partial, spread, running, outgoing, incoming,
    gram_buf, square_row, square_col, order_ref, begin_ref, send_sem, recv_sem,
):
    my_row = lax.axis_index("row")
    my_col = lax.axis_index("col")
    tile_rows, slots, size = entries_ref.shape[:3]
    stored = tile_rows * slots
    order = now_ref.shape[0]
    share = now_ref.shape[1] // size
    half = n_row // 2
    started = []

    def row_peer(m):
        return flipped(my_row, m, n_row)

    def col_peer(m):
        return flipped(my_col, m, n_col)

    barrier = pltpu.get_barrier_semaphore()
    for m in range(1, n_row):
        pl.semaphore_signal(barrier, inc=1, device_id=(row_peer(m), my_col), device_id_type=MESH)
    for m in range(1, n_col):
        pl.semaphore_signal(barrier, inc=1, device_id=(my_row, col_peer(m)), device_id_type=MESH)

    def send(step, phase, k, source, target, device):
        copy = pltpu.make_async_remote_copy(
            src_ref=source, dst_ref=target,
            send_sem=send_sem.at[step, phase, k], recv_sem=recv_sem.at[step, phase, k],
            device_id=device, device_id_type=MESH,
        )
        copy.start()
        started.append(copy)
        return copy

    def tiles_of(values):
        return [values[:, t * size : (t + 1) * size] for t in range(share)]

    def load(ref):
        return tiles_of(near(ref[...].astype(jnp.float32)))

    def block(full, row):
        return full.at[pl.ds(row * share, share)]

    current, earlier, earliest = load(now_ref), load(prev_ref), load(prev2_ref)
    gram_old = near(gram_ref[...].astype(jnp.float32))
    square_old = near(square_ref[...].astype(jnp.float32))
    inverse_old = near(inverse_ref[...].astype(jnp.float32))
    inverse_older = near(inverse2_ref[...].astype(jnp.float32))
    identity = identity_of(order)
    for t in range(share):
        full_a[my_row * share + t] = current[t]
    pl.semaphore_wait(barrier, n_row + n_col - 2)

    def gather_start(step, full):
        mine = block(full, my_row)
        copies = [
            send(step, GATHER, m, mine, mine, (row_peer(2 * m), my_col)) for m in range(1, half)
        ]
        copies.append(send(step, GATHER, 0, mine, mine, (row_peer(1), my_col)))
        return copies

    def gather_finish(step, full, copies):
        passed = []
        for m in range(1, half):
            copies[m - 1].wait_recv()
            got = block(full, row_peer(2 * m))
            passed.append(send(step, GATHER, half + m, got, got, (row_peer(1), my_col)))
        copies[-1].wait_recv()
        for copy in passed:
            copy.wait_recv()

    def third_of():
        middle = near(identity - small_product(inverse_old, gram_old))
        return -small_product(
            small_product(near(square_old + gram_old), middle), inverse_older
        )

    gathers = gather_start(0, full_a)
    for i in range(stored):
        tile16[i] = entries_ref[i // slots, i % slots].astype(jnp.float32).astype(jnp.bfloat16)
    cols = [cols_ref[i // slots, i % slots] for i in range(stored)]

    def as_int(flag):
        return jnp.where(flag, 1, 0).astype(jnp.int32)

    ranks = []
    for i in range(stored):
        rank = jnp.int32(0)
        for j in range(stored):
            if j != i:
                rank = rank + as_int(cols[j] <= cols[i] if j < i else cols[j] < cols[i])
        ranks.append(rank)
    for k in range(stored):
        place = jnp.int32(0)
        for i in range(1, stored):
            place = place + jnp.where(ranks[i] == k, i, 0).astype(jnp.int32)
        order_ref[k] = place

    def count(tile, carry):
        below = jnp.int32(0)
        for i in range(stored):
            below = below + as_int(cols[i] < tile)
        begin_ref[tile] = below
        return carry

    lax.fori_loop(0, n_row * share + 1, count, 0)
    third = third_of()
    gather_finish(0, full_a, gathers)

    def forward(step, full):
        copies = []
        for r in range(tile_rows):
            total = None
            for s in range(slots):
                picked = full[cols[r * slots + s]]
                term = dot_t(digits(picked), tile16[r * slots + s])
                total = term if total is None else total + term
            partial[step, my_col, r] = fold_two(total[:order], total[order:])
            own = partial.at[step, my_col, r]
            for m in range(1, n_col):
                copies.append(
                    send(step, PARTIAL, r * n_col + m, own, own, (my_row, col_peer(m)))
                )
        return copies

    def summed_partial(step, r):
        total = partial[step, 0, r]
        for c in range(1, n_col):
            total = total + partial[step, c, r]
        return total

    sends = forward(0, full_a)
    for copy in sends:
        copy.wait_recv()
    projected = [near(summed_partial(0, r)) for r in range(tile_rows)]

    for step in range(2):
        gram_buf[step, my_row] = pack(gram_tiles(projected))
        own = gram_buf.at[step, my_row]
        grams = [send(step, GRAM, m, own, own, (row_peer(m), my_col)) for m in range(1, n_row)]

        for r in range(tile_rows):
            both = digits(projected[r])
            for s in range(slots):
                spread[r * slots + s] = dot(both, tile16[r * slots + s])
        total = jnp.zeros((2 * order, size), jnp.float32)
        running[0] = total
        for i in range(stored):
            total = total + spread[order_ref[i]]
            running[i + 1] = total
        def finish_block(peer):
            for t in range(share):
                tile = peer * share + t
                summed = running[begin_ref[tile + 1]] - running[begin_ref[tile]]
                outgoing[step, tile] = fold_two(summed[:order], summed[order:])

        across = {}
        for m in range(half - 1, -1, -1):
            peer = row_peer(2 * m + 1)
            finish_block(peer)
            across[m] = send(
                step, SCATTER, m, block(outgoing.at[step], peer),
                incoming.at[step, m], (row_peer(1), my_col),
            )
        for m in range(half - 1, -1, -1):
            finish_block(row_peer(2 * m))
        scatters = []
        for m in range(half - 1, 0, -1):
            across[m].wait_recv()
            peer = row_peer(2 * m)
            for t in range(share):
                outgoing[step, peer * share + t] = (
                    outgoing[step, peer * share + t] + incoming[step, m, t]
                )
            scatters.append(
                send(
                    step, SCATTER, half + m, block(outgoing.at[step], peer),
                    incoming.at[step, half + m], (peer, my_col),
                )
            )
        scatters.append(across[0])

        for copy in grams:
            copy.wait_recv()
        total = gram_buf[step, 0]
        for r in range(1, n_row):
            total = total + gram_buf[step, r]
        gram_now = unpack(near(total))
        inverse_now = inverse_of(gram_now)
        second = -small_product(gram_now, inverse_old)
        if step:
            third = third_of()
        parts = []
        for t in range(share):
            one = product_parts(second, earlier[t])
            two = product_parts(third, earliest[t])
            upper, mid, lower = [a + b for a, b in zip(one, two)]
            parts.append(near(upper) * 15.0 + near(mid) * 256.0 + lower)

        for copy in scatters:
            copy.wait_recv()
        applied = []
        for t in range(share):
            total = outgoing[step, my_row * share + t]
            for m in [0] + list(range(half + 1, n_row)):
                total = total + incoming[step, m, t]
            applied.append(near(total))

        ready = [near(applied[t] + parts[t]) for t in range(share)]
        if step == 0:
            for t in range(share):
                full_b[my_row * share + t] = ready[t]
            gathers = gather_start(1, full_b)

        square_row[step, my_row] = pack(gram_tiles(applied))
        own = square_row.at[step, my_row]
        squares = [
            send(step, SQUARE_ROW, m, own, own, (row_peer(m), my_col)) for m in range(1, n_row)
        ]
        if step == 0:
            gather_finish(1, full_b, gathers)
            sends = forward(1, full_b)
        for copy in squares:
            copy.wait_recv()
        total = square_row[step, 0]
        for r in range(1, n_row):
            total = total + square_row[step, r]
        square_col[step, my_col] = near(total)
        own = square_col.at[step, my_col]
        squares = [
            send(step, SQUARE_COL, m, own, own, (my_row, col_peer(m))) for m in range(1, n_col)
        ]
        for copy in squares:
            copy.wait_recv()
        total = square_col[step, 0]
        for c in range(1, n_col):
            total = total + square_col[step, c]
        square_now = unpack(near(total))

        first = near(identity - small_product(near(square_now + gram_now), inverse_now))
        if step == 0:
            rest = [fold_three(*product_parts(first, projected[r])) for r in range(tile_rows)]
            for copy in sends:
                copy.wait_recv()
            projected = [near(summed_partial(1, r) + rest[r]) for r in range(tile_rows)]
        following = []
        for t in range(share):
            upper, mid, lower = product_parts(first, current[t])
            following.append(
                whole(ready[t] + near(upper) * 15.0 + near(mid) * 256.0 + lower)
            )
        out = (next_ref, later_ref)[step]
        for t in range(share):
            out[:, t * size : (t + 1) * size] = following[t]
        earliest, earlier, current = earlier, current, [near(f) for f in following]
        inverse_older, inverse_old = inverse_old, inverse_now
        gram_old, square_old = gram_now, square_now

    for copy in started:
        copy.wait_send()


def body(
    n_row, n_col, entries, tile_cols, block_now, block_prev, block_prev2,
    gram_prev, square_prev, inverse_prev, inverse_prev2,
):
    tile_rows, slots, size = entries.shape[:3]
    order, width = block_now.shape
    share = width // size
    col_tiles = n_row * share
    stored = tile_rows * slots
    assert tile_rows <= 4 and share <= 4 and n_row % 2 == 0

    copies = max(n_row + 1, tile_rows * n_col)
    f32 = jnp.float32
    smem = pl.BlockSpec(memory_space=pltpu.SMEM)
    vmem = pl.BlockSpec(memory_space=pltpu.VMEM)
    packed = (order // 4, order * 4)
    following, later = pl.pallas_call(
        functools.partial(kernel, n_row, n_col),
        out_shape=(jax.ShapeDtypeStruct((order, width), f32),) * 2,
        in_specs=[smem] + [vmem] * 8,
        out_specs=(vmem, vmem),
        scratch_shapes=[
            pltpu.VMEM((stored, size, size), jnp.bfloat16),
            pltpu.VMEM((col_tiles, order, size), f32),
            pltpu.VMEM((col_tiles, order, size), f32),
            pltpu.VMEM((2, n_col, tile_rows, order, size), f32),
            pltpu.VMEM((stored, 2 * order, size), f32),
            pltpu.VMEM((stored + 1, 2 * order, size), f32),
            pltpu.VMEM((2, col_tiles, order, size), f32),
            pltpu.VMEM((2, n_row, share, order, size), f32),
            pltpu.VMEM((2, n_row) + packed, f32),
            pltpu.VMEM((2, n_row) + packed, f32),
            pltpu.VMEM((2, n_col) + packed, f32),
            pltpu.SMEM((stored,), jnp.int32),
            pltpu.SMEM((col_tiles + 1,), jnp.int32),
            pltpu.SemaphoreType.DMA((2, 6, copies)),
            pltpu.SemaphoreType.DMA((2, 6, copies)),
        ],
        compiler_params=pltpu.CompilerParams(collective_id=0, has_side_effects=True),
    )(
        tile_cols, entries, block_now, block_prev, block_prev2,
        gram_prev, square_prev, inverse_prev, inverse_prev2,
    )
    return following / modulus, later / modulus


def solution(mesh):
    placed = (
        P("row", "col", None, None),
        P("row", "col"),
        P(None, ("col", "row")),
        P(None, ("col", "row")),
        P(None, ("col", "row")),
        P(),
        P(),
        P(),
        P(),
    )
    return jax.shard_map(
        functools.partial(body, mesh.shape["row"], mesh.shape["col"]),
        mesh=mesh,
        in_specs=placed,
        out_specs=(P(None, ("col", "row")), P(None, ("col", "row"))),
        check_vma=False,
    )
```

profile of v0, /device:TPU:0, one launch (start us, length us, event | category | flops | bytes accessed | tf_op | source)
XLA Modules:
  0.0 74.6 jit_solution(16819790293528847349)
XLA Ops:
  0.6 72.5 %shard_map.104 = (f32[32,512]{1,0:T(8,128)}, f32[32,512]{1,0:T(8,128)}) custom-call(s32[4,4]{1,0:T(4,128)} %cols_ref.1, s32[4,4,128,128]{3,2,1,0:T(8,128)} %entries_ref.1, s32[32,512]{1,0:T(8,128)} %now_ref.1, s32[32,512]{1,0:T(8,128)} %prev_ref.1, s32[32,512]{1,0:T(8,128)} %prev2_ref.1, s32[32,32]{1,0:T(8,128)} %gram_ref.1, s32[32,32]{1,0:T(8,128)} %square_ref.1, ...), custom_call_target="tpu_custom_call" | custom-call | tf_op jit(solution)/shard_map/pallas_call | solution.py:430
  73.1 1.5 %broadcast_multiply_fusion = (f32[32,512]{1,0:T(8,128)}, f32[32,512]{1,0:T(8,128)}) fusion(f32[32,512]{1,0:T(8,128)} %get-tuple-element.5, f32[32,512]{1,0:T(8,128)} %get-tuple-element.4), kind=kLoop, calls=%fused_computation | loop fusion | flops 32768 | bytes 262144 | tf_op jit(solution)/shard_map/div | solution.py:457
where the time goes:
time: 74.8 us; the launch traced here: 74.6 us
  Pallas kernels  72.5 us (97%)
  other arithmetic  1.53 us (2%)
    pallas_call x1, Pallas kernels, body(): pl.pallas_call(functools.partial(kernel, n_row, n_col), out_shape=(jax.Sh...  72.5 us
    div x1, other arithmetic, body(): return (following / modulus, later / modulus)  1.53 us

commit v1 on v0

v1 whole, which is shorter than its diff:
```python
import functools

import jax
import jax.numpy as jnp
from jax import lax
from jax.experimental import pallas as pl
from jax.experimental.pallas import tpu as pltpu
from jax.sharding import PartitionSpec as P

modulus = 65521.0
reciprocal = 1.0 / 65521.0
MESH = pl.DeviceIdType.MESH
CHUNKS = 4
GATHER, PARTIAL, SCATTER, GRAM, SQUARE_ROW, SQUARE_COL = range(6)


def near(values):
    return values - jnp.floor(values * reciprocal + 0.5) * modulus


def whole(values):
    signed = near(values)
    return jnp.where(signed < 0.0, signed + modulus, signed)


def split(values):
    top = jnp.floor(values * (1.0 / 256.0) + 0.5)
    return top, values - top * 256.0


def digits(values):
    top, low = split(values)
    return jnp.concatenate([top, low], axis=0).astype(jnp.bfloat16)


def fold_two(top, low):
    return near(near(top) * 256.0 + low)


def fold_three(upper, middle, lower):
    return near(near(upper) * 15.0 + near(middle) * 256.0 + near(lower))


def mulmod(left, right):
    top, low = split(right)
    return near(near(left * top) * 256.0 + left * low)


def dot(left, right):
    return jnp.dot(left, right, preferred_element_type=jnp.float32)


def dot_t(left, right):
    return lax.dot_general(
        left, right, (((1,), (1,)), ((), ())), preferred_element_type=jnp.float32
    )


def product_parts(left, right):
    order = left.shape[0]
    left_digits = digits(left)
    right_top, right_low = split(right)
    with_top = dot(left_digits, right_top.astype(jnp.bfloat16))
    with_low = dot(left_digits, right_low.astype(jnp.bfloat16))
    return with_top[:order], with_top[order:] + with_low[:order], with_low[order:]


def small_product(left, right):
    return fold_three(*product_parts(left, right))


def gram_tiles(tiles):
    order = tiles[0].shape[0]
    total = None
    for tile in tiles:
        both = digits(tile)
        term = dot_t(both, both)
        total = term if total is None else total + term
    return fold_three(
        total[:order, :order],
        total[:order, order:] + total[order:, :order],
        total[order:, order:],
    )


def power_inverse(number):
    result = None
    square = number
    for position in range(16):
        if 65519 >> position & 1:
            result = square if result is None else mulmod(result, square)
        if position < 15:
            square = mulmod(square, square)
    return result


def identity_of(order):
    rows = lax.broadcasted_iota(jnp.int32, (order, order), 0)
    lanes = lax.broadcasted_iota(jnp.int32, (order, order), 1)
    return jnp.where(rows == lanes, 1.0, 0.0).astype(jnp.float32)


def inverse_of(matrix):
    order = matrix.shape[0]
    work = jnp.concatenate([matrix, identity_of(order)], axis=1)
    rows = lax.broadcasted_iota(jnp.int32, (order, 1), 0)
    for column in range(order):
        entry = work[:, column : column + 1]
        usable = (entry != 0.0) & (rows >= column)
        first = jnp.min(jnp.where(usable, rows, order), axis=0, keepdims=True)
        chosen = rows == jnp.where(first == order, column, first)
        pivot_row = jnp.sum(jnp.where(chosen, work, 0.0), axis=0, keepdims=True)
        pivot = jnp.sum(jnp.where(chosen, entry, 0.0), axis=0, keepdims=True)
        swapped = jnp.where(chosen, work[column : column + 1, :], work)
        factor = jnp.where(chosen, entry[column : column + 1, :], entry)
        pivot_row = jnp.where(pivot == 0.0, 0.0, pivot_row)
        pivot = jnp.where(pivot == 0.0, 1.0, pivot)
        pivot_top, pivot_low = split(pivot)
        factor_top, factor_low = split(factor)
        upper = near(pivot_top * swapped - factor_top * pivot_row)
        reduced = near(upper * 256.0 + (pivot_low * swapped - factor_low * pivot_row))
        work = jnp.where(rows == column, pivot_row, reduced)
    left = work[:, :order]
    diagonal = jnp.sum(left * identity_of(order), axis=1, keepdims=True)
    return mulmod(work[:, order:], power_inverse(diagonal))


def pack(values):
    rows = values.shape[0] // 4
    return jnp.concatenate([values[g * rows : (g + 1) * rows] for g in range(4)], axis=1)


def unpack(values):
    width = values.shape[1] // 4
    return jnp.concatenate([values[:, g * width : (g + 1) * width] for g in range(4)], axis=0)


def flipped(place, mask, count):
    assert count & (count - 1) == 0
    bit = 1
    moved = place
    while bit < count:
        if mask & bit:
            moved = moved + bit - 2 * bit * lax.rem(place // bit, 2)
        bit *= 2
    return moved


def kernel(
    n_row, n_col, chunks, plan, cols_any, entries_any, now_any, prev_any, prev2_any,
    gram_any, square_any, inverse_any, inverse2_any, next_ref, later_ref,
    cols_ref, entries_ref, blocks, smalls, tile16, full_a, full_b, partial, folded, running,
    outgoing, incoming, gram_buf, square_row, square_col, order_ref, begin_ref,
    local_sem, send_sem, recv_sem,
):
    my_row = lax.axis_index("row")
    my_col = lax.axis_index("col")
    tile_rows, slots, size = entries_ref.shape[:3]
    stored = tile_rows * slots
    order, width = blocks.shape[1:]
    rows = order // chunks
    share = width // size
    half = n_row // 2

    def row_peer(m):
        return flipped(my_row, m, n_row)

    def col_peer(m):
        return flipped(my_col, m, n_col)

    barrier = pltpu.get_barrier_semaphore()
    for m in range(1, n_row):
        pl.semaphore_signal(barrier, inc=1, device_id=(row_peer(m), my_col), device_id_type=MESH)
    for m in range(1, n_col):
        pl.semaphore_signal(barrier, inc=1, device_id=(my_row, col_peer(m)), device_id_type=MESH)

    inputs = [
        (now_any, blocks.at[0]), (cols_any, cols_ref), (entries_any, entries_ref),
        (gram_any, smalls.at[0]), (square_any, smalls.at[1]),
        (inverse_any, smalls.at[2]), (inverse2_any, smalls.at[3]),
        (prev_any, blocks.at[1]), (prev2_any, blocks.at[2]),
    ]
    loads = [
        pltpu.make_async_copy(source, target, local_sem.at[k])
        for k, (source, target) in enumerate(inputs)
    ]
    for copy in loads:
        copy.start()

    def sem_of(key):
        return plan.setdefault(key, len(plan))

    sent = {}

    def send(kind, key, source, target, device):
        sent[kind] = sent.get(kind, 0) + 1
        pltpu.make_async_remote_copy(
            src_ref=source, dst_ref=target,
            send_sem=send_sem.at[kind], recv_sem=recv_sem.at[sem_of(key)],
            device_id=device, device_id_type=MESH,
        ).start()

    def received(key, ref):
        pltpu.make_async_copy(ref, ref, recv_sem.at[sem_of(key)]).wait()

    def row_device(m):
        return (row_peer(m), my_col)

    def tiles_of(values):
        return [values[:, t * size : (t + 1) * size] for t in range(share)]

    def cut(values, c):
        return values[c * rows : (c + 1) * rows]

    def join(parts):
        return parts[0] if len(parts) == 1 else jnp.concatenate(parts, axis=0)

    def small(k):
        return near(smalls[k].astype(jnp.float32))

    identity = identity_of(order)

    def block(full, c, row):
        return full[c].at[pl.ds(row * share, share)]

    def gather_start(full, c):
        mine = block(full, c, my_row)
        send(GATHER, ("across", c), mine, mine, row_device(1))
        for m in range(1, half):
            send(GATHER, ("along", c, m), mine, mine, row_device(2 * m))

    def gather_relay(full, c):
        for m in range(1, half):
            got = block(full, c, row_peer(2 * m))
            received(("along", c, m), got)
            send(GATHER, ("across", c), got, got, row_device(1))

    def gather_finish(full, c):
        received(("across", c), full[c].at[pl.ds(0, half * share)])

    loads[0].wait()
    current = tiles_of(near(blocks[0].astype(jnp.float32)))
    for c in range(chunks):
        for t in range(share):
            full_a[c][my_row * share + t] = cut(current[t], c)
    pl.semaphore_wait(barrier, n_row + n_col - 2)
    for c in range(chunks):
        gather_start(full_a, c)

    loads[2].wait()
    for i in range(stored):
        tile16[i] = entries_ref[i // slots, i % slots].astype(jnp.float32).astype(jnp.bfloat16)
    loads[1].wait()
    cols = [cols_ref[i // slots, i % slots] for i in range(stored)]

    def as_int(flag):
        return jnp.where(flag, 1, 0).astype(jnp.int32)

    def sort_slots():
        ranks = []
        for i in range(stored):
            rank = jnp.int32(0)
            for j in range(stored):
                if j != i:
                    rank = rank + as_int(cols[j] <= cols[i] if j < i else cols[j] < cols[i])
            ranks.append(rank)
        for k in range(stored):
            place = jnp.int32(0)
            for i in range(1, stored):
                place = place + jnp.where(ranks[i] == k, i, 0).astype(jnp.int32)
            order_ref[k] = place

        def count(tile, carry):
            below = jnp.int32(0)
            for i in range(stored):
                below = below + as_int(cols[i] < tile)
            begin_ref[tile] = below
            return carry

        lax.fori_loop(0, n_row * share + 1, count, 0)

    for c in range(chunks):
        gather_relay(full_a, c)

    def forward(step, full, c):
        base = (step * chunks + c) * n_col
        for r in range(tile_rows):
            total = None
            for s in range(slots):
                picked = full[c][cols[r * slots + s]]
                term = dot_t(digits(picked), tile16[r * slots + s])
                total = term if total is None else total + term
            partial[base + my_col, :, r * size : (r + 1) * size] = fold_two(
                total[:rows], total[rows:]
            )
        own = partial.at[base + my_col]
        for m in range(1, n_col):
            send(PARTIAL, ("partial", step, c), own, own, (my_row, col_peer(m)))

    def summed_partial(step, c):
        base = (step * chunks + c) * n_col
        received(("partial", step, c), partial.at[pl.ds(base, n_col - 1)])
        total = partial[base]
        for k in range(1, n_col):
            total = total + partial[base + k]
        return [total[:, r * size : (r + 1) * size] for r in range(tile_rows)]

    def reduce_small(kind, key, buffer, base, count, place, value, devices):
        buffer[base + place] = value
        own = buffer.at[base + place]
        for device in devices:
            send(kind, key, own, own, device)

        def finish():
            received(key, buffer.at[pl.ds(base, count - 1)])
            total = buffer[base]
            for k in range(1, count):
                total = total + buffer[base + k]
            return near(total)

        return finish

    def gram_start(step, projected):
        return reduce_small(
            GRAM, ("gram",), gram_buf, step * n_row, n_row, my_row,
            pack(gram_tiles(projected)), [row_device(m) for m in range(1, n_row)],
        )

    def scatter_start(step, c, projected):
        for r in range(tile_rows):
            both = digits(projected[r])
            for s in range(slots):
                product = dot(both, tile16[r * slots + s])
                folded[c * stored + r * slots + s] = fold_two(product[:rows], product[rows:])
        total = jnp.zeros((rows, size), jnp.float32)
        first_sum = c * (stored + 1)
        running[first_sum] = total
        for i in range(stored):
            total = total + folded[c * stored + order_ref[i]]
            running[first_sum + i + 1] = total

        def finish_block(peer):
            for t in range(share):
                tile = peer * share + t
                outgoing[(step * chunks + c) * n_row + peer, :, t * size : (t + 1) * size] = (
                    running[first_sum + begin_ref[tile + 1]] - running[first_sum + begin_ref[tile]]
                )

        for m in range(half - 1, -1, -1):
            peer = row_peer(2 * m + 1)
            finish_block(peer)
            send(
                SCATTER, ("scatter", c, m), outgoing.at[(step * chunks + c) * n_row + peer],
                incoming.at[(step * chunks + c) * n_row + m], row_device(1),
            )
        for m in range(half - 1, -1, -1):
            finish_block(row_peer(2 * m))

    def scatter_relay(step, c):
        base = (step * chunks + c) * n_row
        for m in range(half - 1, 0, -1):
            got = incoming.at[base + m]
            received(("scatter", c, m), got)
            own = outgoing.at[base + row_peer(2 * m)]
            own[...] = own[...] + got[...]
            send(
                SCATTER, ("scattered", c), own, incoming.at[base + half + m], row_device(2 * m)
            )

    def scatter_finish(step, c):
        base = (step * chunks + c) * n_row
        received(("scatter", c, 0), incoming.at[base])
        received(("scattered", c), incoming.at[pl.ds(base + half + 1, half - 1)])
        total = outgoing[base + my_row] + incoming[base]
        for m in range(half + 1, n_row):
            total = total + incoming[base + m]
        return tiles_of(near(total))

    def square_start(step, applied):
        return reduce_small(
            SQUARE_ROW, ("square_row",), square_row, step * n_row, n_row, my_row,
            pack(gram_tiles(applied)), [row_device(m) for m in range(1, n_row)],
        )

    def square_pass(step, value):
        return reduce_small(
            SQUARE_COL, ("square_col", step), square_col, step * n_col, n_col, my_col,
            value, [(my_row, col_peer(m)) for m in range(1, n_col)],
        )

    def third_of(square_old, gram_old, inverse_old, inverse_older):
        middle = near(identity - small_product(inverse_old, gram_old))
        return -small_product(
            small_product(near(square_old + gram_old), middle), inverse_older
        )

    def parts_of(second, third, earlier, earliest):
        parts = []
        for t in range(share):
            one = product_parts(second, earlier[t])
            two = product_parts(third, earliest[t])
            upper, mid, lower = [a + b for a, b in zip(one, two)]
            parts.append(near(upper) * 15.0 + near(mid) * 256.0 + lower)
        return parts

    def advance(out, first, ready, current):
        following = []
        for t in range(share):
            upper, mid, lower = product_parts(first, current[t])
            value = whole(ready[t] + near(upper) * 15.0 + near(mid) * 256.0 + lower)
            out[:, t * size : (t + 1) * size] = value
            following.append(value)
        return following

    def joined(pieces):
        return [join([piece[k] for piece in pieces]) for k in range(len(pieces[0]))]

    for c in range(chunks):
        gather_finish(full_a, c)
        forward(0, full_a, c)
    sort_slots()
    for copy in loads[3:]:
        copy.wait()
    earlier = tiles_of(near(blocks[1].astype(jnp.float32)))
    earliest = tiles_of(near(blocks[2].astype(jnp.float32)))
    gram_old, square_old, inverse_old, inverse_older = [small(k) for k in range(4)]

    pieces = []
    for c in range(chunks):
        pieces.append([near(v) for v in summed_partial(0, c)])
        if c == chunks - 1:
            projected = joined(pieces)
            gram_finish = gram_start(0, projected)
        scatter_start(0, c, pieces[c])
    third = third_of(square_old, gram_old, inverse_old, inverse_older)
    for c in range(chunks):
        scatter_relay(0, c)
    gram_now = unpack(gram_finish())
    second = -small_product(gram_now, inverse_old)
    parts = parts_of(second, third, earlier, earliest)
    applied_pieces, ready_pieces = [], []
    for c in range(chunks):
        applied = scatter_finish(0, c)
        ready = [near(applied[t] + cut(parts[t], c)) for t in range(share)]
        for t in range(share):
            full_b[c][my_row * share + t] = ready[t]
        gather_start(full_b, c)
        applied_pieces.append(applied)
        ready_pieces.append(ready)
        if c == 0:
            inverse_now = inverse_of(gram_now)
    ready = joined(ready_pieces)
    square_finish = square_start(0, joined(applied_pieces))
    for c in range(chunks):
        gather_relay(full_b, c)
    square_finish = square_pass(0, square_finish())
    for c in range(chunks):
        gather_finish(full_b, c)
        forward(1, full_b, c)
    square_now = unpack(square_finish())
    first = near(identity - small_product(near(square_now + gram_now), inverse_now))
    rest = [fold_three(*product_parts(first, projected[r])) for r in range(tile_rows)]

    pieces = []
    for c in range(chunks):
        pieces.append(
            [near(v + cut(rest[r], c)) for r, v in enumerate(summed_partial(1, c))]
        )
        if c == chunks - 1:
            gram_finish = gram_start(1, joined(pieces))
        scatter_start(1, c, pieces[c])
    following = [near(v) for v in advance(next_ref, first, ready, current)]
    third = third_of(square_now, gram_now, inverse_now, inverse_old)
    for c in range(chunks):
        scatter_relay(1, c)
    gram_last = unpack(gram_finish())
    inverse_last = inverse_of(gram_last)
    second = -small_product(gram_last, inverse_now)
    parts = parts_of(second, third, current, earlier)
    applied = joined([scatter_finish(1, c) for c in range(chunks)])
    square_finish = square_start(1, applied)
    ready = [applied[t] + parts[t] for t in range(share)]
    square_finish = square_pass(1, square_finish())
    square_last = unpack(square_finish())
    first = near(identity - small_product(near(square_last + gram_last), inverse_last))
    advance(later_ref, first, [near(v) for v in ready], following)

    def all_sent(kind, ref):
        blocks_sent = ref.at[pl.ds(0, sent[kind])]
        pltpu.make_async_copy(blocks_sent, blocks_sent, send_sem.at[kind]).wait()

    all_sent(GATHER, outgoing)
    all_sent(SCATTER, outgoing)
    all_sent(PARTIAL, partial)
    all_sent(GRAM, gram_buf)
    all_sent(SQUARE_ROW, square_row)
    all_sent(SQUARE_COL, square_col)


def body(
    n_row, n_col, entries, tile_cols, block_now, block_prev, block_prev2,
    gram_prev, square_prev, inverse_prev, inverse_prev2,
):
    tile_rows, slots, size = entries.shape[:3]
    order, width = block_now.shape
    share = width // size
    col_tiles = n_row * share
    stored = tile_rows * slots
    half = n_row // 2
    chunks = CHUNKS
    rows = order // chunks
    assert tile_rows <= 4 and share <= 4 and n_row % 2 == 0 and rows % 8 == 0

    f32, i32 = jnp.float32, jnp.int32
    anywhere = pl.BlockSpec(memory_space=pl.ANY)
    vmem = pl.BlockSpec(memory_space=pltpu.VMEM)
    packed = (order // 4, order * 4)
    arrivals = chunks * (2 * half + 3) + 4
    following, later = pl.pallas_call(
        functools.partial(kernel, n_row, n_col, chunks, {}),
        out_shape=(jax.ShapeDtypeStruct((order, width), f32),) * 2,
        in_specs=[anywhere] * 9,
        out_specs=(vmem, vmem),
        scratch_shapes=[
            pltpu.SMEM(tile_cols.shape, i32),
            pltpu.VMEM(entries.shape, i32),
            pltpu.VMEM((3, order, width), i32),
            pltpu.VMEM((4, order, order), i32),
            pltpu.VMEM((stored, size, size), jnp.bfloat16),
            [pltpu.VMEM((col_tiles, rows, size), f32)] * chunks,
            [pltpu.VMEM((col_tiles, rows, size), f32)] * chunks,
            pltpu.VMEM((2 * chunks * n_col, rows, tile_rows * size), f32),
            pltpu.VMEM((chunks * stored, rows, size), f32),
            pltpu.VMEM((chunks * (stored + 1), rows, size), f32),
            pltpu.VMEM((2 * chunks * n_row, rows, width), f32),
            pltpu.VMEM((2 * chunks * n_row, rows, width), f32),
            pltpu.VMEM((2 * n_row,) + packed, f32),
            pltpu.VMEM((2 * n_row,) + packed, f32),
            pltpu.VMEM((2 * n_col,) + packed, f32),
            pltpu.SMEM((stored,), i32),
            pltpu.SMEM((col_tiles + 1,), i32),
            pltpu.SemaphoreType.DMA((9,)),
            pltpu.SemaphoreType.DMA((6,)),
            pltpu.SemaphoreType.DMA((arrivals,)),
        ],
        compiler_params=pltpu.CompilerParams(collective_id=0, has_side_effects=True),
    )(
        tile_cols, entries, block_now, block_prev, block_prev2,
        gram_prev, square_prev, inverse_prev, inverse_prev2,
    )
    return following / modulus, later / modulus


def solution(mesh):
    placed = (
        P("row", "col", None, None),
        P("row", "col"),
        P(None, ("col", "row")),
        P(None, ("col", "row")),
        P(None, ("col", "row")),
        P(),
        P(),
        P(),
        P(),
    )
    return jax.shard_map(
        functools.partial(body, mesh.shape["row"], mesh.shape["col"]),
        mesh=mesh,
        in_specs=placed,
        out_specs=(P(None, ("col", "row")), P(None, ("col", "row"))),
        check_vma=False,
    )
```

time: 74.8 us -> 63.9 us (0.85)
  Pallas kernels: 72.5 us -> 61.6 us
    pallas_call x1, Pallas kernels: 72.5 us -> 61.6 us  [body(): pl.pallas_call(functools.partial(kernel, n_row, n_col, chunks, {}), out_s...]
where the time goes in v1:
time: 63.9 us; the launch traced here: 63.8 us
  Pallas kernels  61.6 us (96%)
  other arithmetic  1.53 us (2%)
  between operations  0.64 us (1%)
    pallas_call x1, Pallas kernels, body(): pl.pallas_call(functools.partial(kernel, n_row, n_col, chunks, {}), out_s...  61.6 us
    div x1, other arithmetic, body(): return (following / modulus, later / modulus)  1.53 us

profile of v1, /device:TPU:0, one launch (start us, length us, event | category | flops | bytes accessed | tf_op | source)
XLA Modules:
  0.0 63.8 jit_solution(2504056389983598386)
XLA Ops:
  0.6 61.6 %shard_map.104 = (f32[32,512]{1,0:T(8,128)}, f32[32,512]{1,0:T(8,128)}) custom-call(s32[4,4]{1,0:T(4,128)} %cols_any.1, s32[4,4,128,128]{3,2,1,0:T(8,128)} %entries_any.1, s32[32,512]{1,0:T(8,128)} %now_any.1, s32[32,512]{1,0:T(8,128)} %prev_any.1, s32[32,512]{1,0:T(8,128)} %prev2_any.1, s32[32,32]{1,0:T(8,128)} %gram_any.1, s32[32,32]{1,0:T(8,128)} %square_any.1, ...), custom_call_target="tpu_custom_call" | custom-call | tf_op jit(solution)/shard_map/pallas_call | solution.py:519
  62.2 1.5 %broadcast_multiply_fusion = (f32[32,512]{1,0:T(8,128)}, f32[32,512]{1,0:T(8,128)}) fusion(f32[32,512]{1,0:T(8,128)} %get-tuple-element.5, f32[32,512]{1,0:T(8,128)} %get-tuple-element.4), kind=kLoop, calls=%fused_computation | loop fusion | flops 32768 | bytes 262144 | tf_op jit(solution)/shard_map/div | solution.py:551
